TPU v7x, 128 devices: a whole 4x4x4 slice. The times are simulated.
128 devices in a mesh: blk: 128 (over x, z, y, core).
Axes of the slice: x: 4, y: 4, z: 4, core: 2. Of those that a mesh axis runs over, the one named last changes fastest.
Arguments:
- locations: float32 [2, 32768], P(None, 'blk'), may hold values from 0 to 1
- neighbors: int32 [4, 256], P(None, 'blk'), may hold values from -1 to 255, as said below
- noise_precision: float32 [32768], P('blk'), may hold values from 0.5 to 4
- right_side: float32 [16, 32768], P(None, 'blk'), may hold values from -6 to 6
Outputs:
- solution: float32 [16, 32768], P(None, 'blk')
- residual: float32 [16, 32768], P(None, 'blk')
Inputs may be any that keep to these rules, and one draw needn't show every extreme that they name: `neighbors`: entry [k, b] names a block that block b conditions on; the named blocks of one column are distinct and earlier than b, -1 marks an unused slot and used slots come first. Slot 0 names b - 1 for every b > 0. Among all blocks named by the columns of the 2 blocks of one device, at most one block of any other device appears, and every device but the first names one block of the device before it.
All inputs are finite; a program needn't handle non-finite values.
Results may differ from a plain program's by a relative error of at most 0.0003.
Values sent between devices are 32-bit elements; how exact they have to be, the bound alone decides.
No kernel may reach another device: no remote copies, remote signals or barrier semaphores. Data moves between devices by JAX's collectives and lax.ppermute only.
A program may use at most 64 MiB of HBM per device.

v0:
```python
import jax
import jax.numpy as jnp
from jax import lax
from jax.sharding import PartitionSpec as P

BS = 128
KMAX = 4
RHS = 16
ITERS = 2


corr_range = 0.4
nugget = 0.2


def covariance(first_pts, second_pts):
    diff_x = first_pts[0][:, None] - second_pts[0][None, :]
    diff_y = first_pts[1][:, None] - second_pts[1][None, :]
    return jnp.exp(-jnp.sqrt(diff_x * diff_x + diff_y * diff_y) / corr_range)


def build_block(own_pts, near_pts, used_slot, noise_blk):
    width = near_pts.shape[0] * near_pts.shape[2]
    gathered = jnp.transpose(near_pts, (1, 0, 2)).reshape(2, width)
    point_mask = jnp.repeat(used_slot, near_pts.shape[2])
    eye_c = jnp.eye(width, dtype=jnp.float32)
    eye_b = jnp.eye(own_pts.shape[1], dtype=jnp.float32)
    cov_cc = covariance(gathered, gathered) * point_mask[:, None] * point_mask[None, :]
    cov_cc = cov_cc + eye_c * (nugget * point_mask + 1.0 - point_mask)[None, :]
    cov_cb = covariance(gathered, own_pts) * point_mask[:, None]
    cov_bb = covariance(own_pts, own_pts) + nugget * eye_b
    chol_c = jnp.linalg.cholesky(cov_cc)
    first = lax.linalg.triangular_solve(chol_c, cov_cb, left_side=True, lower=True)
    coefficient = lax.linalg.triangular_solve(
        chol_c, first, left_side=True, lower=True, transpose_a=True
    )
    schur = cov_bb - jnp.dot(first.T, first, precision=lax.Precision.HIGHEST)
    chol_low = jnp.linalg.cholesky(schur)
    inv_low = lax.linalg.triangular_solve(chol_low, eye_b, left_side=True, lower=True)
    factor = jnp.dot(inv_low, coefficient.T, precision=lax.Precision.HIGHEST)
    gram_blk = eye_b + jnp.dot(
        chol_low.T * noise_blk[None, :], chol_low, precision=lax.Precision.HIGHEST
    )
    chol_gram = jnp.linalg.cholesky(gram_blk)
    half_root = lax.linalg.triangular_solve(chol_gram, chol_low.T, left_side=True, lower=True)
    precond_blk = jnp.dot(half_root.T, half_root, precision=lax.Precision.HIGHEST)
    return (inv_low, factor, precond_blk)


def per_device(locations, neighbors, noise_precision, right_side):
    local_blocks = neighbors.shape[1]
    points = jnp.transpose(locations.reshape(2, local_blocks, BS), (1, 0, 2))
    block_ids = neighbors.T
    in_use = block_ids >= 0
    safe_ids = jnp.where(in_use, block_ids, 0)
    used_slot = in_use.astype(jnp.float32)
    noise_blk = noise_precision.reshape(local_blocks, BS)
    flat_ids = safe_ids.reshape(-1)
    everything = lax.all_gather(points, "blk", axis=0, tiled=True)
    near_points = everything[safe_ids]

    def one_block(packed):
        return build_block(packed[0], packed[1], packed[2], packed[3])

    inv_low, factor, precond_blk = lax.map(one_block, (points, near_points, used_slot, noise_blk))
    factor_four = factor.reshape(local_blocks, BS, KMAX, BS)

    def condition(vector):
        return jnp.einsum("bri,bij->brj", vector, precond_blk, precision=lax.Precision.HIGHEST)

    def local_dot(left, right):
        return jnp.sum(left * right, axis=(0, 2))

    def residual_dot(left, right):
        return lax.psum(local_dot(left, right), "blk")

    residual = jnp.transpose(right_side.reshape(RHS, local_blocks, BS), (1, 0, 2))
    solution = jnp.zeros_like(residual)
    smoothed = condition(residual)
    direction = smoothed
    res_dot = residual_dot(residual, smoothed)
    for step in range(ITERS):
        every_vec = lax.all_gather(direction, "blk", axis=0, tiled=True)
        near_vec = every_vec[safe_ids]
        whitened = jnp.einsum("bij,brj->bri", inv_low, direction, precision=lax.Precision.HIGHEST)
        whitened = whitened - jnp.einsum(
            "bikj,bkrj->bri", factor_four, near_vec, precision=lax.Precision.HIGHEST
        )
        own_term = jnp.einsum("bri,bij->brj", whitened, inv_low, precision=lax.Precision.HIGHEST)
        back_terms = -jnp.einsum(
            "bri,bikj->bkrj", whitened, factor_four, precision=lax.Precision.HIGHEST
        )
        back_terms = back_terms * used_slot[:, :, None, None]
        flat_terms = back_terms.reshape(local_blocks * KMAX, RHS * BS)
        select = (
            flat_ids[:, None]
            == jnp.arange(local_blocks * lax.axis_size("blk"), dtype=jnp.int32)[None, :]
        ).astype(jnp.float32)
        returned = lax.psum_scatter(
            jnp.dot(select.T, flat_terms, precision=lax.Precision.HIGHEST).reshape(
                local_blocks * lax.axis_size("blk"), RHS, BS
            ),
            "blk",
            scatter_dimension=0,
            tiled=True,
        )
        image = own_term + returned + noise_blk[:, None, :] * direction
        step_size = res_dot / lax.psum(local_dot(direction, image), "blk")
        solution = solution + step_size[None, :, None] * direction
        residual = residual - step_size[None, :, None] * image
        if step + 1 < ITERS:
            smoothed = condition(residual)
            new_dot = residual_dot(residual, smoothed)
            direction = smoothed + (new_dot / res_dot)[None, :, None] * direction
            res_dot = new_dot
    solution = jnp.transpose(solution, (1, 0, 2)).reshape(RHS, local_blocks * BS)
    residual = jnp.transpose(residual, (1, 0, 2)).reshape(RHS, local_blocks * BS)
    return (solution, residual)


def solution(mesh):
    in_specs = (P(None, "blk"), P(None, "blk"), P("blk"), P(None, "blk"))
    out_specs = (P(None, "blk"), P(None, "blk"))
    return jax.shard_map(
        per_device, mesh=mesh, in_specs=in_specs, out_specs=out_specs, check_vma=False
    )
```

profile of v0, /device:TPU:1, one launch (start us, length us, event | category | flops | bytes accessed | tf_op | source)
XLA Modules:
  0.0 2071.3 jit_solution(8483620995492849789)
XLA Ops:
  8.7 38.8 %all_gather.9 = f32[256,2,128]{2,1,0:T(2,128)S(1)} all-gather(f32[2,2,128]{2,1,0:T(2,128)} %bitcast.355), channel_id=1, replica_groups=mesh['blk'=128] {'blk'}, dimensions={0}, use_global_device_ids=true | all-gather | bytes 264192 | tf_op jit(solution)/shard_map/all_gather | solution.py:59
  48.1 393.3 %while.17 = (s32[]{:T(128)}, f32[2,128,128]{2,1,0:T(8,128)S(1)}, f32[2,128,512]{2,1,0:T(8,128)S(1)}, f32[2,128,128]{2,1,0:T(8,128)S(1)}, f32[2,2,128]{2,1,0:T(2,...) while((s32[]{:T(128)}, f32[2,128,128]{2,1,0:T(8,128)S(1)}, ...), condition=%wide.region_11.14_spmd, body=%wide.region_0.13_spmd.sunk | while | flops 1218218240 | bytes 16303054 | solution.py:65
  51.5 11.7 cholesky.521
  63.6 9.8 custom-call.57
  74.2 12.3 cholesky.524
  86.8 9.8 custom-call.58
  99.2 11.7 cholesky.526
  112.6 9.8 custom-call.59
  123.0 11.9 cholesky.527
  136.6 10.5 while.18
  147.1 40.1 %custom-call.61 = f32[4,128,128]{1,2,0:T(8,128)S(1)} custom-call(f32[4,128,128]{2,1,0:T(8,128)} %get-tuple-element.225), custom_call_target="InvertDiagBlocksLowerTriangular" | custom-call | tf_op jit(solution)/shard_map/while/body/eval_jaxpr/triangular_solve | solution.py:33
  191.9 11.7 cholesky.531
  205.4 11.7 cholesky.532
  218.6 10.0 custom-call.63
  244.6 11.7 cholesky.521
  256.6 9.8 custom-call.57
  267.3 11.9 cholesky.524
  291.9 11.7 cholesky.526
  305.3 9.8 custom-call.59
  315.7 11.9 cholesky.527
  329.3 10.5 while.18
  339.8 40.1 %custom-call.61 = f32[4,128,128]{1,2,0:T(8,128)S(1)} custom-call(f32[4,128,128]{2,1,0:T(8,128)} %get-tuple-element.225), custom_call_target="InvertDiagBlocksLowerTriangular" | custom-call | tf_op jit(solution)/shard_map/while/body/eval_jaxpr/triangular_solve | solution.py:33
  384.6 11.7 cholesky.531
  398.1 11.7 cholesky.532
  411.3 10.2 custom-call.63
  442.4 63.4 %all-gather.3.cloned.1.call-done = f32[256,16,128]{2,1,0:T(8,128)} async-done(((f32[2,16,128]{2,1,0:T(8,128)}), f32[256,16,128]{2,1,0:T(8,128)}) %all-gather.3.cloned.1.call-update) | async-done | bytes 2097168 | tf_op jit(solution)/shard_map/all_gather | solution.py:83
  513.6 637.5 %reduce-scatter.3.cloned.1.call-done = f32[2,16,128]{2,1,0:T(8,128)} async-done(((f32[256,16,128]{2,1,0:T(8,128)}), f32[2,16,128]{2,1,0:T(8,128)}) %reduce-scatter.3.cloned.1.call-update) | async-done | bytes 16400 | tf_op jit(solution)/shard_map/reduce_scatter | solution.py:99
  1152.2 69.2 %all-reduce.1 = (f32[16]{0:T(128)S(1)}, f32[16]{0:T(128)S(1)}) all-reduce(f32[16]{0:T(128)S(1)} %get-tuple-element.60, f32[16]{0:T(128)S(1)} %get-tuple-element.59), channel_id=1, replica_groups=mesh['blk'=128] {'blk'}, use_global_device_ids=true, to_apply=%region_13.16 | all-reduce | flops 32 | bytes 256 | tf_op jit(solution)/shard_map/psum | solution.py:75
  1221.8 62.5 %psum.30 = f32[16]{0:T(128)S(1)} all-reduce(f32[16]{0:T(128)S(1)} %get-tuple-element.108), channel_id=1, replica_groups=mesh['blk'=128] {'blk'}, use_global_device_ids=true, to_apply=%region_18.21 | all-reduce | flops 16 | bytes 128 | tf_op jit(solution)/shard_map/psum | solution.py:75
  1285.0 63.1 %all-gather.5.cloned.1.call-done = f32[256,16,128]{2,1,0:T(8,128)} async-done(((f32[2,16,128]{2,1,0:T(8,128)}), f32[256,16,128]{2,1,0:T(8,128)}) %all-gather.5.cloned.1.call-update) | async-done | bytes 2097168 | tf_op jit(solution)/shard_map/all_gather | solution.py:83
  1355.9 637.7 %reduce-scatter.5.cloned.1.call-done = f32[2,16,128]{2,1,0:T(8,128)} async-done(((f32[256,16,128]{2,1,0:T(8,128)}), f32[2,16,128]{2,1,0:T(8,128)}) %reduce-scatter.5.cloned.1.call-update) | async-done | bytes 16400 | tf_op jit(solution)/shard_map/reduce_scatter | solution.py:99
  1994.6 69.2 %psum.31 = f32[16]{0:T(128)S(1)} all-reduce(f32[16]{0:T(128)S(1)} %get-tuple-element.110), channel_id=1, replica_groups=mesh['blk'=128] {'blk'}, use_global_device_ids=true, to_apply=%region_21.24 | all-reduce | flops 16 | bytes 128 | tf_op jit(solution)/shard_map/psum | solution.py:108
  (216 shorter events, 110.8 us)
Async XLA Ops:
  7.2 434.2 %copy-start = (f32[16,256]{1,0:T(8,128)S(1)}, f32[16,256]{1,0:T(8,128)}, u32[]{:S(2)}) copy-start(f32[16,256]{1,0:T(8,128)} %param.12) | copy-start | bytes 49156
  7.2 498.6 %all-gather.3.cloned.1.call-start = ((), (), s32[]{:S(2)}) async-start(), calls=%async_computation.2 | async-start | bytes 2113536 | tf_op jit(solution)/shard_map/all_gather | solution.py:83
  442.2 708.9 %reduce-scatter.3.cloned.1.call-start = ((), (), s32[]{:S(2)}) async-start(), calls=%async_computation.3 | async-start | bytes 2113536 | tf_op jit(solution)/shard_map/reduce_scatter | solution.py:99
  513.6 637.6 %copy-start.1 = (f32[2,128,16]{1,2,0:T(8,128)S(1)}, f32[2,128,16]{1,2,0:T(8,128)}, u32[]{:S(2)}) copy-start(f32[2,128,16]{1,2,0:T(8,128)} %fusion.108) | copy-start | bytes 49156
  513.6 637.6 %copy-start.3 = (f32[2,128]{1,0:T(2,128)S(1)}, f32[2,128]{1,0:T(2,128)}, u32[]{:S(2)}) copy-start(f32[2,128]{1,0:T(2,128)} %get-tuple-element.302) | copy-start | bytes 3076
  513.6 834.5 %all-gather.5.cloned.1.call-start = ((), (), s32[]{:S(2)}) async-start(), calls=%async_computation.4 | async-start | bytes 2113536 | tf_op jit(solution)/shard_map/all_gather | solution.py:83
  1284.9 708.6 %reduce-scatter.5.cloned.1.call-start = ((), (), s32[]{:S(2)}) async-start(), calls=%async_computation.5 | async-start | bytes 2113536 | tf_op jit(solution)/shard_map/reduce_scatter | solution.py:99
  1355.8 637.7 %copy-start.2 = (f32[2,16,128]{2,1,0:T(8,128)S(1)}, f32[2,16,128]{2,1,0:T(8,128)}, u32[]{:S(2)}) copy-start(f32[2,16,128]{2,1,0:T(8,128)} %multiply_add_fusion) | copy-start | bytes 49156
Sparse Core Ops, SparseCore 0:
  442.4 63.3 all-gather.2
  513.7 637.3 reduce-scatter.2
  1285.1 62.9 all-gather.4
  1356.0 637.5 reduce-scatter.4
where the time goes:
time: 2070 us
  waiting for transfers between devices  1400 us (68%)
  other arithmetic  338 us (16%)
  blocking collectives  240 us (12%)
  local copies, waits for them, and re-layouts  36 us (2%)
  matrix products  27.8 us (1%)
    reduce_scatter x2, waiting for transfers between devices, per_device(): lax.psum_scatter(jnp.dot(select.T, flat_terms, precision=lax.Precision.HI...  1280 us
    another operation x28, other arithmetic, build_block(): chol_c = jnp.linalg.cholesky(cov_cc)  159 us
    psum x2, blocking collectives, residual_dot(): return lax.psum(local_dot(left, right), 'blk')  132 us
    all_gather x2, waiting for transfers between devices, per_device(): every_vec = lax.all_gather(direction, 'blk', axis=0, tiled=True)  126 us
    another operation x6, other arithmetic, build_block(): lax.linalg.triangular_solve(chol_c, cov_cb, left_side=True, lower=True)  80.5 us
    psum x1, blocking collectives, per_device(): step_size = res_dot / lax.psum(local_dot(direction, image), 'blk')  69.2 us
  transfers between devices with their start and end apart: 4, of which 4 were waited for; matrix products, arithmetic and copies ran while one was open for 0% of the time, Pallas kernels for 0%

commit v1 on v0

v1 whole, which is shorter than its diff:
```python
import jax
import jax.numpy as jnp
from jax import lax
from jax.experimental import pallas as pl
from jax.experimental.pallas import tpu as pltpu
from jax.sharding import PartitionSpec as P

BS = 128
KMAX = 4
RHS = 16
NDEV = 128
f32 = jnp.float32
HI = lax.Precision.HIGHEST
VM = pl.BlockSpec(memory_space=pltpu.VMEM)
SM = pl.BlockSpec(memory_space=pltpu.SMEM)


def call(body, shapes, n_in, scratch=(), name=None, smem=0, limit=32):
    return pl.pallas_call(
        body,
        in_specs=[SM] * smem + [VM] * (n_in - smem),
        out_specs=[VM] * len(shapes),
        out_shape=[jax.ShapeDtypeStruct(s, f32) for s in shapes],
        scratch_shapes=list(scratch),
        compiler_params=pltpu.CompilerParams(vmem_limit_bytes=limit * 2**20),
        name=name,
    )


def dg(a,b,ca,cb):
    return lax.dot_general(a,b,(((ca,),(cb,)),((),())),precision=HI,preferred_element_type=f32)
def mm(a,b): return dg(a,b,1,0)
def mm_nt(a,b): return dg(a,b,1,1)
def mm_tn(a,b): return dg(a,b,0,0)

def chol_inverse(T, ms, put, SP=32):
    lane=lax.broadcasted_iota(jnp.int32,(8,128),1)
    sub=lax.broadcasted_iota(jnp.int32,(8,128),0)
    NP=SP//8
    for s in range(0,128,SP):
        fin=[[None]*NP for _ in ms]
        R=[[T[m,s+8*q:s+8*q+8,:] for q in range(NP)] for m in ms]
        for q in range(NP):
            base=s+8*q
            inblk=(lane>=base)&(lane<base+8)
            for n in range(len(ms)):
                W=R[n][q]
                C=[jnp.broadcast_to(W[:,base+j:base+j+1],(8,128)) for j in range(8)]
                F=W
                for j in range(8):
                    at=lane==base+j; row=sub==j
                    d=jnp.broadcast_to(C[j][j:j+1],(8,128))
                    r=1.0/d
                    unit=jnp.where(at,1.0,jnp.broadcast_to(W[j:j+1],(8,128)))
                    F=jnp.where(row,unit*lax.rsqrt(d),F)
                    if q<NP-1:
                        pr=unit*r
                        W=jnp.where(row,pr,jnp.where(at,0.0,W)-C[j]*pr)
                        ls=range(j+1,8)
                    else:
                        mul=jnp.where(sub>j,C[j]*r,0.0)
                        W=jnp.where(at&(sub>j),0.0,W)-mul*unit
                        ls=range(j+1,8)
                    for l in ls:
                        e=jnp.broadcast_to(C[l][j:j+1],(8,128))*r
                        C[l]=C[l]-C[j]*e if q==NP-1 else jnp.where(row,e,C[l]-C[j]*e)
                fin[n][q]=F
                put(ms[n],base,jnp.where(lane<=sub+base,F,0.0))
                if q<NP-1:
                    Yr=[jnp.broadcast_to(W[j:j+1],(8,128)) for j in range(8)]
                    for o in range(q+1,NP):
                        A=R[n][o]
                        acc=jnp.where(inblk,0.0,A)
                        for j in range(8):
                            acc=acc-jnp.broadcast_to(A[:,base+j:base+j+1],(8,128))*Yr[j]
                        R[n][o]=acc
        if s+SP<128:
            lane2=lax.broadcasted_iota(jnp.int32,(128-s-SP,128),1)
            ins=(lane2>=s)&(lane2<s+SP)
            for n,m in enumerate(ms):
                F=jnp.concatenate(fin[n],0)
                own=s+lax.broadcasted_iota(jnp.int32,(SP,128),0)
                lf=lax.broadcasted_iota(jnp.int32,(SP,128),1)
                U=mm_tn(F,jnp.where((lf<=own)|(lf>=s+SP),F,0.0))
                T[m,s+SP:,:]=jnp.where(ins,0.0,T[m,s+SP:,:])-U[s+SP:,:]

def cov(xc,yc,xr,yr):
    dx=xc-xr; dy=yc-yr
    return jnp.exp(jnp.sqrt(dx*dx+dy*dy)*(-2.5))

def slot(nbr,k,b):
    ident=nbr[k,b]; used=ident>=0; safe=jnp.where(used,ident,0)
    return used,safe//2,safe%2

def factor_body(nbr, recv0, loc, noise, rhs, coef, g4, gd, d0, send, X, T, G):
    i0=lax.broadcasted_iota(jnp.int32,(128,128),0); i1=lax.broadcasted_iota(jnp.int32,(128,128),1)
    eye=jnp.where(i0==i1,1.0,0.0).astype(f32)
    for b in range(2):
        xs=[];ys=[];ms=[]
        for k in range(4):
            used,dev,which=slot(nbr,k,b)
            xs.append(recv0[pl.ds(5*dev+which,1),:]); ys.append(recv0[pl.ds(5*dev+which+2,1),:])
            ms.append(jnp.where(used,1.0,0.0).astype(f32))
        xs.append(loc[0:1,b*128:(b+1)*128]); ys.append(loc[1:2,b*128:(b+1)*128]); ms.append(jnp.float32(1.0))
        xt=jnp.transpose(jnp.concatenate(xs+[xs[4]]*3,0)); yt=jnp.transpose(jnp.concatenate(ys+[ys[4]]*3,0))
        for k in range(5):
            xc=jnp.broadcast_to(xt[:,k:k+1],(128,128)); yc=jnp.broadcast_to(yt[:,k:k+1],(128,128))
            for l in range(k+1):
                c=cov(xc,yc,xs[l],ys[l])
                if k<4 or l<4: c=c*(ms[k]*ms[l])
                if k==l: c=c+eye*(0.2*ms[k]+1.0-ms[k])
                X[b,k*128:(k+1)*128,l*128:(l+1)*128]=c
    T[0]=X[0,0:128,0:128]; T[1]=X[1,0:128,0:128]
    def stage(k,_):
        def put(m,row,v): G[k,m,row:row+8,:]=v
        chol_inverse(T,[0,1],put)
        for kk in range(4):
            @pl.when(k==kk)
            def _():
                lo=(kk+1)*128
                for b in range(2):
                    L=mm_nt(X[b,lo:,kk*128:lo],G[kk,b])
                    X[b,lo:,kk*128:lo]=L
                    for j in range(kk+1,5):
                        o=j*128
                        v=X[b,o:,o:o+128]-mm_nt(L[o-lo:],L[o-lo:o-lo+128])
                        if j==kk+1: T[b]=v[:128]
                        X[b,o:,o:o+128]=v
        return 0
    lax.fori_loop(0,4,stage,0)
    dn=[]
    for b in range(2):
        d=1.0/noise[0:1,b*128:(b+1)*128]; dn.append(d)
        T[2+b]=T[b]+eye*d
    def put4(m,row,v):
        if m<2: g4[m,row:row+8,:]=v
        else: gd[m-2,row:row+8,:]=v
    chol_inverse(T,[0,1,2,3],put4)
    ds=[]
    for b in range(2):
        cs=[None]*4
        for k in (3,2,1,0):
            e=X[b,512:,k*128:(k+1)*128]
            for j in range(k+1,4):
                e=e-mm(cs[j],X[b,j*128:(j+1)*128,k*128:(k+1)*128])
            cs[k]=mm(e,G[k,b])
            coef[b,:,k*128:(k+1)*128]=cs[k]
        w=rhs[:,b*128:(b+1)*128]*dn[b]
        d=w-mm(mm_nt(w,gd[b]),gd[b])*dn[b]
        d0[b]=d
        ds.append(d)
    def pack(j,_):
        flag=recv0[pl.ds(5*j+4,1),:]
        send[pl.ds(pl.multiple_of(RHS*j,RHS),RHS),:]=jnp.where(flag==1.0,ds[1],ds[0])
        return 0
    lax.fori_loop(0,NDEV,pack,0,unroll=8)


def each(n, body, unroll=8):
    def step(j, carry):
        body(j)
        return carry

    lax.fori_loop(0, n, step, 0, unroll=unroll)


def announce_body(nbr, loc, out):
    rows = jnp.concatenate(
        [loc[0:1, 0:BS], loc[0:1, BS:], loc[1:2, 0:BS], loc[1:2, BS:], jnp.full((1, BS), -1.0, f32)], 0
    )

    def put(j):
        out[pl.ds(5 * j, 5), :] = rows

    each(NDEV, put)
    for b in range(2):
        for k in range(KMAX):
            used, dev, which = slot(nbr, k, b)

            @pl.when(used)
            def _():
                out[pl.ds(5 * dev + 4, 1), :] = jnp.full((1, BS), which.astype(f32), f32)


def apply_body(rows, nbr, v, recv, coef, g4, noise, *rest):
    if rows == RHS:
        q_out, part_out, send = rest
        send[...] = jnp.zeros((NDEV * RHS, BS), f32)
    else:
        parts, q_out, send = rest
    part = jnp.zeros((RHS, BS), f32)
    backs = []
    slots = [[slot(nbr, k, b) for k in range(KMAX)] for b in range(2)]
    for b in range(2):
        near = jnp.concatenate([recv[pl.ds(pl.multiple_of(RHS * s[1], 8), RHS), :] for s in slots[b]], 1)
        own = v[b]
        t = mm_nt(own - mm_nt(near, coef[b]), g4[b])
        q = mm(t, g4[b])
        part = part + t * t + noise[0:1, b * BS : (b + 1) * BS] * own * own
        q_out[b] = q
        backs.append(-mm(q, coef[b]))
    if rows == RHS:
        part_out[...] = part
    else:
        lane = lax.broadcasted_iota(jnp.int32, (RHS, BS), 1)
        sub = lax.broadcasted_iota(jnp.int32, (RHS, BS), 0)
        z = jnp.zeros((RHS, BS), f32)
        for c, val in enumerate((parts[0], parts[1], parts[2], part)):
            z = z + jnp.where(lane == c * RHS + sub, jnp.sum(val, axis=1, keepdims=True), 0.0)
        msg = jnp.concatenate([jnp.zeros((RHS, BS), f32), jnp.sum(z, axis=0, keepdims=True)], 0)

        def put(j):
            send[pl.ds(rows * j, rows), :] = msg

        each(NDEV, put)
    for b in range(2):
        for k in range(KMAX):
            used, dev, _ = slots[b][k]

            @pl.when(used)
            def _():
                at = pl.ds(rows * dev, RHS)
                send[at, :] = send[at, :] + backs[b][:, k * BS : (k + 1) * BS]


def returned(rows, recv0, recv):
    def step(j, acc):
        flag = recv0[pl.ds(5 * j + 4, 1), :]
        msg = recv[pl.ds(rows * j, RHS), :]
        out = [a + jnp.where(flag == float(w), msg, 0.0) for w, a in enumerate(acc[:2])]
        if rows > RHS:
            out.append(acc[2] + recv[pl.ds(rows * j + RHS, 1), :])
        return tuple(out)

    init = (jnp.zeros((RHS, BS), f32), jnp.zeros((RHS, BS), f32))
    if rows > RHS:
        init = init + (jnp.zeros((1, BS), f32),)
    return lax.fori_loop(0, NDEV, step, init, unroll=8)


def middle_body(recv0, recv, q, d0, noise, rhs, gd, apart, im0, y, parts, send):
    ret = returned(RHS, recv0, recv)
    rz = jnp.zeros((RHS, BS), f32)
    bb = jnp.zeros((RHS, BS), f32)
    ys = []
    for b in range(2):
        s = slice(b * BS, (b + 1) * BS)
        d = d0[b]
        im = q[b] + ret[b] + noise[0:1, s] * d
        dn = 1.0 / noise[0:1, s]
        w = im * dn
        yb = w - mm(mm_nt(w, gd[b]), gd[b]) * dn
        im0[b] = im
        y[b] = yb
        ys.append(yb)
        bb = bb + im * yb
        rz = rz + rhs[:, s] * d
    parts[0] = rz
    parts[1] = apart[...]
    parts[2] = bb

    def put(j):
        flag = recv0[pl.ds(5 * j + 4, 1), :]
        send[pl.ds(pl.multiple_of(RHS * j, RHS), RHS), :] = jnp.where(flag == 1.0, ys[1], ys[0])

    each(NDEV, put)


def last_body(recv0, recv, q1, y, d0, im0, noise, rhs, sol, res):
    ret = returned(RHS + 1, recv0, recv)
    lane = lax.broadcasted_iota(jnp.int32, (RHS, BS), 1)
    sub = lax.broadcasted_iota(jnp.int32, (RHS, BS), 0)
    rz, a, bb, cc = [
        jnp.sum(jnp.where(lane == c * RHS + sub, ret[2], 0.0), axis=1, keepdims=True) for c in range(4)
    ]
    al0 = rz / a
    new = al0 * al0 * bb - rz
    grow = 1.0 + new / rz
    al1 = new / (al0 * al0 * cc - grow * grow * a)
    for b in range(2):
        s = slice(b * BS, (b + 1) * BS)
        w = q1[b] + ret[b] + noise[0:1, s] * y[b]
        sol[:, s] = al0 * d0[b] + al1 * (grow * d0[b] - al0 * y[b])
        res[:, s] = rhs[:, s] - al0 * im0[b] - al1 * (grow * im0[b] - al0 * w)


def per_device(locations, neighbors, noise_precision, right_side):
    noise = noise_precision.reshape(1, 2 * BS)
    blk = (2, RHS, BS)
    sq = (2, BS, BS)

    def exchange(msg, rows):
        out = lax.all_to_all(msg.reshape(NDEV, 1, rows * BS), "blk", 0, 0, tiled=True)
        return out.reshape(NDEV * rows, BS)

    (send0,) = call(announce_body, [(NDEV * 5, BS)], 2, smem=1, name="announce")(neighbors, locations)
    recv0 = exchange(send0, 5)
    coef, g4, gd, d0, send1 = call(
        factor_body,
        [(2, BS, KMAX * BS), sq, sq, blk, (NDEV * RHS, BS)],
        5,
        smem=1,
        scratch=[pltpu.VMEM((2, 640, 640), f32), pltpu.VMEM((4, BS, BS), f32), pltpu.VMEM((4, 2, BS, BS), f32)],
        name="factor",
    )(neighbors, recv0, locations, noise, right_side)
    recv1 = exchange(send1, RHS)
    q0, apart, send2 = call(
        lambda *r: apply_body(RHS, *r), [blk, (RHS, BS), (NDEV * RHS, BS)], 6, smem=1, name="apply_first"
    )(neighbors, d0, recv1, coef, g4, noise)
    recv2 = exchange(send2, RHS)
    im0, y, parts, send3 = call(
        middle_body, [blk, blk, (3, RHS, BS), (NDEV * RHS, BS)], 8, name="middle"
    )(recv0, recv2, q0, d0, noise, right_side, gd, apart)
    recv3 = exchange(send3, RHS)
    q1, send4 = call(
        lambda *r: apply_body(RHS + 1, *r), [blk, (NDEV * (RHS + 1), BS)], 7, smem=1, name="apply_second"
    )(neighbors, y, recv3, coef, g4, noise, parts)
    recv4 = exchange(send4, RHS + 1)
    return tuple(
        call(last_body, [(RHS, 2 * BS)] * 2, 8, name="last")(
            recv0, recv4, q1, y, d0, im0, noise, right_side
        )
    )


def solution(mesh):
    in_specs = (P(None, "blk"), P(None, "blk"), P("blk"), P(None, "blk"))
    out_specs = (P(None, "blk"), P(None, "blk"))
    return jax.shard_map(
        per_device, mesh=mesh, in_specs=in_specs, out_specs=out_specs, check_vma=False
    )
```

time: 2070 us -> 167 us (0.08)
  waiting for transfers between devices: 1400 us -> 0 us
  other arithmetic: 338 us -> 0 us
  blocking collectives: 240 us -> 118 us
  Pallas kernels: 0 us -> 44.8 us
  local copies, waits for them, and re-layouts: 36 us -> 3.53 us
  matrix products: 27.8 us -> 0 us
    reduce_scatter x2 -> x0, waiting for transfers between devices: 1280 us -> none  [per_device(): lax.psum_scatter(jnp.dot(select.T, flat_terms, precision=lax.Precision.HI...]
    another operation x56 -> x0, other arithmetic: 331 us -> none  [the longest x28 159 us: build_block(): chol_c = jnp.linalg.cholesky(cov_cc)]
    psum x3 -> x0, blocking collectives: 201 us -> none  [the longest x2 132 us: residual_dot(): return lax.psum(local_dot(left, right), 'blk')]
    all_gather x2 -> x0, waiting for transfers between devices: 126 us -> none  [per_device(): every_vec = lax.all_gather(direction, 'blk', axis=0, tiled=True)]
    all_to_all x0 -> x5, blocking collectives: none -> 118 us  [exchange(): lax.all_to_all(msg.reshape(NDEV, 1, rows * BS), 'blk', 0, 0, tiled=True)]
    pallas_call x0 -> x6, Pallas kernels: none -> 44.8 us  [the longest x1 35.6 us: per_device(): call(factor_body, [(2, BS, KMAX * BS), sq, sq, blk, (NDEV * RHS, BS)], 5,...]
    all_gather x1 -> x0, blocking collectives: 38.8 us -> none  [per_device(): everything = lax.all_gather(points, 'blk', axis=0, tiled=True)]
    another operation x54 -> x0, local copies, waits for them, and re-layouts: 22.6 us -> none
  transfers between devices with their start and end apart: 4 -> 0, of which waited for: 4 -> 0; matrix products, arithmetic and copies ran while one was open for 0% -> 0% of each run, Pallas kernels for 0% -> 0%
where the time goes in v1:
time: 167 us
  blocking collectives  118 us (71%)
  Pallas kernels  44.8 us (27%)
  local copies, waits for them, and re-layouts  3.53 us (2%)
    all_to_all x5, blocking collectives, exchange(): lax.all_to_all(msg.reshape(NDEV, 1, rows * BS), 'blk', 0, 0, tiled=True)  118 us
    pallas_call x1, Pallas kernels, per_device(): call(factor_body, [(2, BS, KMAX * BS), sq, sq, blk, (NDEV * RHS, BS)], 5,...  35.6 us
    unnamed x11, local copies, waits for them, and re-layouts  3.53 us

profile of v1, /device:TPU:1, one launch (start us, length us, event | category | flops | bytes accessed | tf_op | source)
XLA Modules:
  0.0 166.6 jit_solution(10489182509255511214)
XLA Ops:
  0.6 0.8 copy.10.nbr.r_0_
  1.4 0.0 copy-start.3
  1.4 0.7 copy-done.3
  2.1 0.7 announce.1
  2.8 22.7 %all_to_all.25 = f32[128,1,640]{2,1,0:T(1,128)S(1)} all-to-all(f32[128,1,640]{2,1,0:T(1,128)S(1)} %bitcast.18), channel_id=1, replica_groups=mesh['blk'=128] {'blk'}, dimensions={0} | all-to-all | bytes 655360 | tf_op jit(solution)/shard_map/all_to_all | solution.py:293
  25.5 0.0 copy-start
  25.5 0.7 copy-done
  26.2 0.0 copy-start.2
  26.2 0.7 copy-done.2
  26.9 0.0 copy-start.4
  26.9 0.7 copy-done.4
  27.6 35.6 %factor.1 = (f32[2,128,512]{2,1,0:T(8,128)S(1)}, f32[2,128,128]{2,1,0:T(8,128)S(1)}, f32[2,128,128]{2,1,0:T(8,128)S(1)}, f32[2,16,128]{2,1,0:T(8,128)S(1)}, f32[2048,128]{1,0:T(8,128)S(1)}) custom-call(s32[4,2]{1,0:T(4,128)S(1)} %copy.10.nbr.r_0_, f32[640,128]{1,0:T(8,128)S(1)} %bitcast.11, f32[2,256]{1,0:T(2,128)S(1)} %copy-done.4, f32[1,256]{1,0:T(1,128)S(1)} %bitcast.23, ...), custom_call_target="tpu_custom_call" | custom-call | tf_op jit(solution)/shard_map/factor/pallas_call | solution.py:298
  63.2 23.6 %all_to_all.26 = f32[128,1,2048]{2,1,0:T(1,128)S(1)} all-to-all(f32[128,1,2048]{2,1,0:T(1,128)S(1)} %bitcast.21), channel_id=1, replica_groups=mesh['blk'=128] {'blk'}, dimensions={0} | all-to-all | bytes 2097152 | tf_op jit(solution)/shard_map/all_to_all | solution.py:293
  86.8 2.9 %apply_first.1 = (f32[2,16,128]{2,1,0:T(8,128)S(1)}, f32[16,128]{1,0:T(8,128)S(1)}, f32[2048,128]{1,0:T(8,128)S(1)}) custom-call(s32[4,2]{1,0:T(4,128)S(1)} %copy.10.nbr.r_0_, f32[2,16,128]{2,1,0:T(8,128)S(1)} %get-tuple-element.16.r_1_.d0, f32[2048,128]{1,0:T(8,128)S(1)} %bitcast.16, f32[2,128,512]{2,1,0:T(8,128)S(1)} %get-tuple-element.18.r_3_, ...), custom_call_target="tpu_custom_call" | custom-call | tf_op jit(solution)/shard_map/apply_first/pallas_call | solution.py:307
  89.7 0.0 copy-start.1
  89.7 23.6 %all_to_all.27 = f32[128,1,2048]{2,1,0:T(1,128)S(1)} all-to-all(f32[128,1,2048]{2,1,0:T(1,128)S(1)} %bitcast.22), channel_id=1, replica_groups=mesh['blk'=128] {'blk'}, dimensions={0} | all-to-all | bytes 2097152 | tf_op jit(solution)/shard_map/all_to_all | solution.py:293
  113.3 0.0 copy-done.1
  113.3 1.4 middle.1
  114.7 23.5 %all_to_all.28 = f32[128,1,2048]{2,1,0:T(1,128)S(1)} all-to-all(f32[128,1,2048]{2,1,0:T(1,128)S(1)} %bitcast.20), channel_id=1, replica_groups=mesh['blk'=128] {'blk'}, dimensions={0} | all-to-all | bytes 2097152 | tf_op jit(solution)/shard_map/all_to_all | solution.py:293
  138.3 3.1 %apply_second.1 = (f32[2,16,128]{2,1,0:T(8,128)S(1)}, f32[2176,128]{1,0:T(8,128)S(1)}) custom-call(s32[4,2]{1,0:T(4,128)S(1)} %copy.10.nbr.r_0_, f32[2,16,128]{2,1,0:T(8,128)S(1)} %get-tuple-element.24.r_1_.y, f32[2048,128]{1,0:T(8,128)S(1)} %bitcast.15, f32[2,128,512]{2,1,0:T(8,128)S(1)} %get-tuple-element.18.r_3_, ...), custom_call_target="tpu_custom_call" | custom-call | tf_op jit(solution)/shard_map/apply_second/pallas_call | solution.py:315
  141.3 24.2 %all_to_all.29 = f32[128,1,2176]{2,1,0:T(1,128)S(1)} all-to-all(f32[128,1,2176]{2,1,0:T(1,128)S(1)} %bitcast.19), channel_id=1, replica_groups=mesh['blk'=128] {'blk'}, dimensions={0} | all-to-all | bytes 2228224 | tf_op jit(solution)/shard_map/all_to_all | solution.py:293
  165.5 1.1 last.1
Async XLA Ops:
  1.4 0.7 copy-start.3
  25.5 0.7 copy-start
  26.2 0.7 copy-start.2
  26.9 0.7 copy-start.4
  89.7 23.6 %copy-start.1 = (f32[16,256]{1,0:T(8,128)S(1)}, f32[16,256]{1,0:T(8,128)}, u32[]{:S(2)}) copy-start(f32[16,256]{1,0:T(8,128)} %rhs.5) | copy-start | bytes 49156

commit v2 on v1

--- a/solution.py
+++ b/solution.py
@@ -33,7 +33,7 @@
 def mm_nt(a,b): return dg(a,b,1,1)
 def mm_tn(a,b): return dg(a,b,0,0)
 
-def chol_inverse(T, ms, put, SP=32):
+def chol_pieces(T, ms, put, SP=32):
     lane=lax.broadcasted_iota(jnp.int32,(8,128),1)
     sub=lax.broadcasted_iota(jnp.int32,(8,128),0)
     NP=SP//8
@@ -45,7 +45,7 @@
             inblk=(lane>=base)&(lane<base+8)
             for n in range(len(ms)):
                 W=R[n][q]
-                C=[jnp.broadcast_to(W[:,base+j:base+j+1],(8,128)) for j in range(8)]
+                C=[jnp.broadcast_to(jnp.sum(jnp.where(lane==base+j,W,0.0),axis=1,keepdims=True),(8,128)) for j in range(8)]
                 F=W
                 for j in range(8):
                     at=lane==base+j; row=sub==j
@@ -72,8 +72,9 @@
                         A=R[n][o]
                         acc=jnp.where(inblk,0.0,A)
                         for j in range(8):
-                            acc=acc-jnp.broadcast_to(A[:,base+j:base+j+1],(8,128))*Yr[j]
+                            acc=acc-jnp.broadcast_to(jnp.sum(jnp.where(lane==base+j,A,0.0),axis=1,keepdims=True),(8,128))*Yr[j]
                         R[n][o]=acc
+            yield
         if s+SP<128:
             lane2=lax.broadcasted_iota(jnp.int32,(128-s-SP,128),1)
             ins=(lane2>=s)&(lane2<s+SP)
@@ -81,71 +82,98 @@
                 F=jnp.concatenate(fin[n],0)
                 own=s+lax.broadcasted_iota(jnp.int32,(SP,128),0)
                 lf=lax.broadcasted_iota(jnp.int32,(SP,128),1)
-                U=mm_tn(F,jnp.where((lf<=own)|(lf>=s+SP),F,0.0))
-                T[m,s+SP:,:]=jnp.where(ins,0.0,T[m,s+SP:,:])-U[s+SP:,:]
+                F2=jnp.where((lf<=own)|(lf>=s+SP),F,0.0)
+                T[m,s+SP:,:]=jnp.where(ins,0.0,T[m,s+SP:,:])-mm(jnp.transpose(F)[s+SP:],F2)
+            yield
+
+def chol_inverse(T, ms, put, fill=(), pieces=19):
+    fill=list(fill)
+    for i,_ in enumerate(chol_pieces(T,ms,put)):
+        take=-(-len(fill)//max(pieces-i,1))
+        for f in fill[:take]: f()
+        fill=fill[take:]
+    for f in fill: f()
 
 def cov(xc,yc,xr,yr):
     dx=xc-xr; dy=yc-yr
     return jnp.exp(jnp.sqrt(dx*dx+dy*dy)*(-2.5))
 
 def slot(nbr,k,b):
-    ident=nbr[k,b]; used=ident>=0; safe=jnp.where(used,ident,0)
+    ident=nbr[b,k]; used=ident>=0; safe=jnp.where(used,ident,0)
     return used,safe//2,safe%2
 
-def factor_body(nbr, recv0, loc, noise, rhs, coef, g4, gd, d0, send, X, T, G):
+def factor_body(nbr_hbm, recv0, own_hbm, fac, g4, gd, d0, send, own, nbr_v, X, T, G, coef, nbr, sems):
+    pairs=[(nbr_hbm,nbr),(own_hbm,own),(nbr_hbm,nbr_v)]
+    copies=[pltpu.make_async_copy(a,b,sems.at[i]) for i,(a,b) in enumerate(pairs)]
+    for c in copies: c.start()
+    for c in copies: c.wait()
     i0=lax.broadcasted_iota(jnp.int32,(128,128),0); i1=lax.broadcasted_iota(jnp.int32,(128,128),1)
     eye=jnp.where(i0==i1,1.0,0.0).astype(f32)
+    early=[]
     for b in range(2):
         xs=[];ys=[];ms=[]
         for k in range(4):
             used,dev,which=slot(nbr,k,b)
             xs.append(recv0[pl.ds(5*dev+which,1),:]); ys.append(recv0[pl.ds(5*dev+which+2,1),:])
             ms.append(jnp.where(used,1.0,0.0).astype(f32))
-        xs.append(loc[0:1,b*128:(b+1)*128]); ys.append(loc[1:2,b*128:(b+1)*128]); ms.append(jnp.float32(1.0))
+        xs.append(own[0:1,b*128:(b+1)*128]); ys.append(own[1:2,b*128:(b+1)*128]); ms.append(jnp.float32(1.0))
         xt=jnp.transpose(jnp.concatenate(xs+[xs[4]]*3,0)); yt=jnp.transpose(jnp.concatenate(ys+[ys[4]]*3,0))
-        for k in range(5):
+        def block(k,l,b=b,xs=xs,ys=ys,ms=ms,xt=xt,yt=yt):
             xc=jnp.broadcast_to(xt[:,k:k+1],(128,128)); yc=jnp.broadcast_to(yt[:,k:k+1],(128,128))
+            c=cov(xc,yc,xs[l],ys[l])
+            if k<4 or l<4: c=c*(ms[k]*ms[l])
+            if k==l: c=c+eye*(0.2*ms[k]+1.0-ms[k])
+            if k==0: T[b]=c
+            else: X[b,k*128:(k+1)*128,l*128:(l+1)*128]=c
+        block(0,0)
+        for k in range(1,5):
             for l in range(k+1):
-                c=cov(xc,yc,xs[l],ys[l])
-                if k<4 or l<4: c=c*(ms[k]*ms[l])
-                if k==l: c=c+eye*(0.2*ms[k]+1.0-ms[k])
-                X[b,k*128:(k+1)*128,l*128:(l+1)*128]=c
-    T[0]=X[0,0:128,0:128]; T[1]=X[1,0:128,0:128]
-    def stage(k,_):
-        def put(m,row,v): G[k,m,row:row+8,:]=v
-        chol_inverse(T,[0,1],put)
-        for kk in range(4):
-            @pl.when(k==kk)
-            def _():
-                lo=(kk+1)*128
-                for b in range(2):
-                    L=mm_nt(X[b,lo:,kk*128:lo],G[kk,b])
-                    X[b,lo:,kk*128:lo]=L
-                    for j in range(kk+1,5):
-                        o=j*128
-                        v=X[b,o:,o:o+128]-mm_nt(L[o-lo:],L[o-lo:o-lo+128])
-                        if j==kk+1: T[b]=v[:128]
-                        X[b,o:,o:o+128]=v
-        return 0
-    lax.fori_loop(0,4,stage,0)
+                early.append(lambda k=k,l=l,block=block: block(k,l))
+    def at(i,j): return (slice(i*128,(i+1)*128),slice(j*128,(j+1)*128))
+    fill=early
+    for k in range(4):
+        def put(m,row,v,k=k): G[k,m,row:row+8,:]=v
+        chol_inverse(T,[0,1],put,fill)
+        fill=[]
+        n=k+1
+        for b in range(2):
+            r,c=at(n,k)
+            L=mm_nt(X[b,r,c],G[k,b])
+            X[b,r,c]=L
+            r,c=at(n,n)
+            T[b]=X[b,r,c]-mm_nt(L,L)
+        for b in range(2):
+            def rest(b=b,k=k,n=n):
+                if n<4:
+                    lo=(n+1)*128
+                    X[b,lo:,k*128:n*128]=mm_nt(X[b,lo:,k*128:n*128],G[k,b])
+            def column(j,b=b,k=k,n=n):
+                lo=max(j,n+1)*128
+                c=slice(k*128,n*128)
+                X[b,lo:,j*128:(j+1)*128]=X[b,lo:,j*128:(j+1)*128]-mm_nt(X[b,lo:,c],X[b,j*128:(j+1)*128,c])
+            if n<4:
+                fill.append(rest)
+                for j in range(n,5): fill.append(lambda j=j,column=column: column(j))
     dn=[]
     for b in range(2):
-        d=1.0/noise[0:1,b*128:(b+1)*128]; dn.append(d)
+        d=1.0/own[2:3,b*128:(b+1)*128]; dn.append(d)
         T[2+b]=T[b]+eye*d
     def put4(m,row,v):
         if m<2: g4[m,row:row+8,:]=v
         else: gd[m-2,row:row+8,:]=v
-    chol_inverse(T,[0,1,2,3],put4)
+    for k in (3,2,1,0):
+        for b in range(2):
+            def term(b=b,k=k):
+                X[b,512:,k*128:(k+1)*128]=X[b,512:,k*128:(k+1)*128]-mm(coef[b,:,(k+1)*128:],X[b,(k+1)*128:512,k*128:(k+1)*128])
+            def close(b=b,k=k):
+                coef[b,:,k*128:(k+1)*128]=mm(X[b,512:,k*128:(k+1)*128],G[k,b])
+            if k<3: fill.append(term)
+            fill.append(close)
+    chol_inverse(T,[0,1,2,3],put4,fill)
     ds=[]
     for b in range(2):
-        cs=[None]*4
-        for k in (3,2,1,0):
-            e=X[b,512:,k*128:(k+1)*128]
-            for j in range(k+1,4):
-                e=e-mm(cs[j],X[b,j*128:(j+1)*128,k*128:(k+1)*128])
-            cs[k]=mm(e,G[k,b])
-            coef[b,:,k*128:(k+1)*128]=cs[k]
-        w=rhs[:,b*128:(b+1)*128]*dn[b]
+        fac[b]=mm(g4[b],coef[b])
+        w=own[8:24,b*128:(b+1)*128]*dn[b]
         d=w-mm(mm_nt(w,gd[b]),gd[b])*dn[b]
         d0[b]=d
         ds.append(d)
@@ -164,7 +192,15 @@
     lax.fori_loop(0, n, step, 0, unroll=unroll)
 
 
-def announce_body(nbr, loc, out):
+def announce_body(nbr_hbm, loc_hbm, noise_hbm, rhs_hbm, out, own, nbr, sems):
+    pairs = [(nbr_hbm, nbr), (loc_hbm, own.at[0:2]), (noise_hbm, own.at[2:3]), (rhs_hbm, own.at[8:24])]
+    copies = [pltpu.make_async_copy(s, d, sems.at[i]) for i, (s, d) in enumerate(pairs)]
+    own[...] = jnp.zeros((24, 2 * BS), f32)
+    for c in copies:
+        c.start()
+    for c in copies:
+        c.wait()
+    loc = own[0:2, :]
     rows = jnp.concatenate(
         [loc[0:1, 0:BS], loc[0:1, BS:], loc[1:2, 0:BS], loc[1:2, BS:], jnp.full((1, BS), -1.0, f32)], 0
     )
@@ -182,7 +218,7 @@
                 out[pl.ds(5 * dev + 4, 1), :] = jnp.full((1, BS), which.astype(f32), f32)
 
 
-def apply_body(rows, nbr, v, recv, coef, g4, noise, *rest):
+def apply_body(rows, nbr, v, recv, fac, g4, args, *rest):
     if rows == RHS:
         q_out, part_out, send = rest
         send[...] = jnp.zeros((NDEV * RHS, BS), f32)
@@ -194,11 +230,11 @@
     for b in range(2):
         near = jnp.concatenate([recv[pl.ds(pl.multiple_of(RHS * s[1], 8), RHS), :] for s in slots[b]], 1)
         own = v[b]
-        t = mm_nt(own - mm_nt(near, coef[b]), g4[b])
+        t = mm_nt(own, g4[b]) - mm_nt(near, fac[b])
         q = mm(t, g4[b])
-        part = part + t * t + noise[0:1, b * BS : (b + 1) * BS] * own * own
+        part = part + t * t + args[2:3, b * BS : (b + 1) * BS] * own * own
         q_out[b] = q
-        backs.append(-mm(q, coef[b]))
+        backs.append(-mm(t, fac[b]))
     if rows == RHS:
         part_out[...] = part
     else:
@@ -238,7 +274,7 @@
     return lax.fori_loop(0, NDEV, step, init, unroll=8)
 
 
-def middle_body(recv0, recv, q, d0, noise, rhs, gd, apart, im0, y, parts, send):
+def middle_body(recv0, recv, q, d0, args, gd, apart, im0, y, parts, send):
     ret = returned(RHS, recv0, recv)
     rz = jnp.zeros((RHS, BS), f32)
     bb = jnp.zeros((RHS, BS), f32)
@@ -246,15 +282,15 @@
     for b in range(2):
         s = slice(b * BS, (b + 1) * BS)
         d = d0[b]
-        im = q[b] + ret[b] + noise[0:1, s] * d
-        dn = 1.0 / noise[0:1, s]
+        im = q[b] + ret[b] + args[2:3, s] * d
+        dn = 1.0 / args[2:3, s]
         w = im * dn
         yb = w - mm(mm_nt(w, gd[b]), gd[b]) * dn
         im0[b] = im
         y[b] = yb
         ys.append(yb)
         bb = bb + im * yb
-        rz = rz + rhs[:, s] * d
+        rz = rz + args[8:24, s] * d
     parts[0] = rz
     parts[1] = apart[...]
     parts[2] = bb
@@ -266,7 +302,7 @@
     each(NDEV, put)
 
 
-def last_body(recv0, recv, q1, y, d0, im0, noise, rhs, sol, res):
+def last_body(recv0, recv, q1, y, d0, im0, args, sol, res):
     ret = returned(RHS + 1, recv0, recv)
     lane = lax.broadcasted_iota(jnp.int32, (RHS, BS), 1)
     sub = lax.broadcasted_iota(jnp.int32, (RHS, BS), 0)
@@ -279,13 +315,12 @@
     al1 = new / (al0 * al0 * cc - grow * grow * a)
     for b in range(2):
         s = slice(b * BS, (b + 1) * BS)
-        w = q1[b] + ret[b] + noise[0:1, s] * y[b]
+        w = q1[b] + ret[b] + args[2:3, s] * y[b]
         sol[:, s] = al0 * d0[b] + al1 * (grow * d0[b] - al0 * y[b])
-        res[:, s] = rhs[:, s] - al0 * im0[b] - al1 * (grow * im0[b] - al0 * w)
+        res[:, s] = args[8:24, s] - al0 * im0[b] - al1 * (grow * im0[b] - al0 * w)
 
 
 def per_device(locations, neighbors, noise_precision, right_side):
-    noise = noise_precision.reshape(1, 2 * BS)
     blk = (2, RHS, BS)
     sq = (2, BS, BS)
 
@@ -293,32 +328,50 @@
         out = lax.all_to_all(msg.reshape(NDEV, 1, rows * BS), "blk", 0, 0, tiled=True)
         return out.reshape(NDEV * rows, BS)
 
-    (send0,) = call(announce_body, [(NDEV * 5, BS)], 2, smem=1, name="announce")(neighbors, locations)
+    hbm = pl.BlockSpec(memory_space=pltpu.HBM)
+    smem = pltpu.SMEM((2, KMAX), jnp.int32)
+    send0, own0 = pl.pallas_call(
+        announce_body,
+        in_specs=[hbm] * 4,
+        out_specs=[VM] * 2,
+        out_shape=[jax.ShapeDtypeStruct(s, f32) for s in ((NDEV * 5, BS), (24, 2 * BS))],
+        scratch_shapes=[smem, pltpu.SemaphoreType.DMA((4,))],
+        name="announce",
+    )(neighbors.T, locations, noise_precision.reshape(1, 2 * BS), right_side)
     recv0 = exchange(send0, 5)
-    coef, g4, gd, d0, send1 = call(
+    shapes = [(2, BS, KMAX * BS), sq, sq, blk, (NDEV * RHS, BS), (24, 2 * BS)]
+    fac, g4, gd, d0, send1, own, nbr = pl.pallas_call(
         factor_body,
-        [(2, BS, KMAX * BS), sq, sq, blk, (NDEV * RHS, BS)],
-        5,
-        smem=1,
-        scratch=[pltpu.VMEM((2, 640, 640), f32), pltpu.VMEM((4, BS, BS), f32), pltpu.VMEM((4, 2, BS, BS), f32)],
+        in_specs=[hbm, VM, hbm],
+        out_specs=[VM] * 7,
+        out_shape=[jax.ShapeDtypeStruct(s, f32) for s in shapes] + [jax.ShapeDtypeStruct((2, KMAX), jnp.int32)],
+        scratch_shapes=[
+            pltpu.VMEM((2, 640, 640), f32),
+            pltpu.VMEM((4, BS, BS), f32),
+            pltpu.VMEM((4, 2, BS, BS), f32),
+            pltpu.VMEM((2, BS, KMAX * BS), f32),
+            smem,
+            pltpu.SemaphoreType.DMA((3,)),
+        ],
+        compiler_params=pltpu.CompilerParams(vmem_limit_bytes=32 * 2**20),
         name="factor",
-    )(neighbors, recv0, locations, noise, right_side)
+    )(neighbors.T, recv0, own0)
     recv1 = exchange(send1, RHS)
     q0, apart, send2 = call(
         lambda *r: apply_body(RHS, *r), [blk, (RHS, BS), (NDEV * RHS, BS)], 6, smem=1, name="apply_first"
-    )(neighbors, d0, recv1, coef, g4, noise)
+    )(nbr, d0, recv1, fac, g4, own)
     recv2 = exchange(send2, RHS)
     im0, y, parts, send3 = call(
-        middle_body, [blk, blk, (3, RHS, BS), (NDEV * RHS, BS)], 8, name="middle"
-    )(recv0, recv2, q0, d0, noise, right_side, gd, apart)
+        middle_body, [blk, blk, (3, RHS, BS), (NDEV * RHS, BS)], 7, name="middle"
+    )(recv0, recv2, q0, d0, own, gd, apart)
     recv3 = exchange(send3, RHS)
     q1, send4 = call(
         lambda *r: apply_body(RHS + 1, *r), [blk, (NDEV * (RHS + 1), BS)], 7, smem=1, name="apply_second"
-    )(neighbors, y, recv3, coef, g4, noise, parts)
+    )(nbr, y, recv3, fac, g4, own, parts)
     recv4 = exchange(send4, RHS + 1)
     return tuple(
-        call(last_body, [(RHS, 2 * BS)] * 2, 8, name="last")(
-            recv0, recv4, q1, y, d0, im0, noise, right_side
+        call(last_body, [(RHS, 2 * BS)] * 2, 7, name="last")(
+            recv0, recv4, q1, y, d0, im0, own
         )
     )
 

time: 167 us -> 156 us (0.934)
  Pallas kernels: 44.8 us -> 35.7 us
  local copies, waits for them, and re-layouts: 3.53 us -> 1.42 us
    pallas_call x4, Pallas kernels: 38.8 us -> 30.9 us  [the longest x1 26.8 us: per_device(): pl.pallas_call(factor_body, in_specs=[hbm, VM, hbm], out_specs=[VM] * 7,...]
    unnamed x11 -> x4, local copies, waits for them, and re-layouts: 3.53 us -> 1.42 us
where the time goes in v2:
time: 156 us
  blocking collectives  118 us (76%)
  Pallas kernels  35.7 us (23%)
    all_to_all x5, blocking collectives, exchange(): lax.all_to_all(msg.reshape(NDEV, 1, rows * BS), 'blk', 0, 0, tiled=True)  118 us
    pallas_call x1, Pallas kernels, per_device(): pl.pallas_call(factor_body, in_specs=[hbm, VM, hbm], out_specs=[VM] * 7,...  26.8 us

profile of v2, /device:TPU:1, one launch (start us, length us, event | category | flops | bytes accessed | tf_op | source)
XLA Modules:
  0.0 155.7 jit_solution(16887399134021229370)
XLA Ops:
  0.6 1.7 %announce.1 = (f32[640,128]{1,0:T(8,128)}, f32[24,256]{1,0:T(8,128)}) custom-call(s32[2,4]{1,0:T(2,128)} %bitcast.23, f32[2,256]{1,0:T(2,128)} %loc_hbm.1, f32[1,256]{1,0:T(1,128)} %bitcast.26, f32[16,256]{1,0:T(8,128)} %rhs_hbm.1), custom_call_target="tpu_custom_call" | custom-call | tf_op jit(solution)/shard_map/announce/pallas_call | solution.py:333
  2.3 22.9 %all_to_all.25 = f32[128,1,640]{2,1,0:T(1,128)S(1)} all-to-all(f32[128,1,640]{2,1,0:T(1,128)} %bitcast.25), channel_id=1, replica_groups=mesh['blk'=128] {'blk'}, dimensions={0} | all-to-all | bytes 655360 | tf_op jit(solution)/shard_map/all_to_all | solution.py:328
  25.2 0.0 copy-start
  25.2 0.7 copy-done
  26.0 0.0 copy-start.1
  26.0 0.7 copy-done.1
  26.6 26.8 %factor.1 = (f32[2,128,512]{2,1,0:T(8,128)S(1)}, f32[2,128,128]{2,1,0:T(8,128)S(1)}, f32[2,128,128]{2,1,0:T(8,128)S(1)}, f32[2,16,128]{2,1,0:T(8,128)S(1)}, f32[...) custom-call(s32[2,4]{1,0:T(2,128)S(1)} %bitcast.24, f32[640,128]{1,0:T(8,128)S(1)} %bitcast.12, ...), custom_call_target="tpu_custom_call" | custom-call | tf_op jit(solution)/shard_map/factor/pallas_call | solution.py:343
  53.4 23.6 %all_to_all.26 = f32[128,1,2048]{2,1,0:T(1,128)S(1)} all-to-all(f32[128,1,2048]{2,1,0:T(1,128)S(1)} %bitcast.20), channel_id=1, replica_groups=mesh['blk'=128] {'blk'}, dimensions={0} | all-to-all | bytes 2097152 | tf_op jit(solution)/shard_map/all_to_all | solution.py:328
  77.0 2.3 %apply_first.1 = (f32[2,16,128]{2,1,0:T(8,128)S(1)}, f32[16,128]{1,0:T(8,128)S(1)}, f32[2048,128]{1,0:T(8,128)S(1)}) custom-call(s32[2,4]{1,0:T(2,128)S(1)} %get-tuple-element.22.r_0_, f32[2,16,128]{2,1,0:T(8,128)S(1)} %get-tuple-element.23.r_1_.d0, f32[2048,128]{1,0:T(8,128)S(1)} %bitcast.18, f32[2,128,512]{2,1,0:T(8,128)S(1)} %get-tuple-element.25.r_3_, ...), custom_call_target="tpu_custom_call" | custom-call | tf_op jit(solution)/shard_map/apply_first/pallas_call | solution.py:360
  79.3 23.6 %all_to_all.27 = f32[128,1,2048]{2,1,0:T(1,128)S(1)} all-to-all(f32[128,1,2048]{2,1,0:T(1,128)S(1)} %bitcast.22), channel_id=1, replica_groups=mesh['blk'=128] {'blk'}, dimensions={0} | all-to-all | bytes 2097152 | tf_op jit(solution)/shard_map/all_to_all | solution.py:328
  102.9 1.4 middle.1
  104.4 23.5 %all_to_all.28 = f32[128,1,2048]{2,1,0:T(1,128)S(1)} all-to-all(f32[128,1,2048]{2,1,0:T(1,128)S(1)} %bitcast.21), channel_id=1, replica_groups=mesh['blk'=128] {'blk'}, dimensions={0} | all-to-all | bytes 2097152 | tf_op jit(solution)/shard_map/all_to_all | solution.py:328
  127.9 2.5 %apply_second.1 = (f32[2,16,128]{2,1,0:T(8,128)S(1)}, f32[2176,128]{1,0:T(8,128)S(1)}) custom-call(s32[2,4]{1,0:T(2,128)S(1)} %get-tuple-element.22.r_0_, f32[2,16,128]{2,1,0:T(8,128)S(1)} %get-tuple-element.32.r_1_.y, f32[2048,128]{1,0:T(8,128)S(1)} %bitcast.17, f32[2,128,512]{2,1,0:T(8,128)S(1)} %get-tuple-element.25.r_3_, ...), custom_call_target="tpu_custom_call" | custom-call | tf_op jit(solution)/shard_map/apply_second/pallas_call | solution.py:368
  130.4 24.2 %all_to_all.29 = f32[128,1,2176]{2,1,0:T(1,128)S(1)} all-to-all(f32[128,1,2176]{2,1,0:T(1,128)S(1)} %bitcast.19), channel_id=1, replica_groups=mesh['blk'=128] {'blk'}, dimensions={0} | all-to-all | bytes 2228224 | tf_op jit(solution)/shard_map/all_to_all | solution.py:328
  154.6 1.1 last.1
Async XLA Ops:
  25.2 0.7 copy-start
  26.0 0.7 copy-start.1

commit v3 on v2

--- a/solution.py
+++ b/solution.py
@@ -31,9 +31,16 @@
     return lax.dot_general(a,b,(((ca,),(cb,)),((),())),precision=HI,preferred_element_type=f32)
 def mm(a,b): return dg(a,b,1,0)
 def mm_nt(a,b): return dg(a,b,1,1)
+def split(a):
+    hi=a.astype(jnp.bfloat16)
+    return hi,(a-hi.astype(f32)).astype(jnp.bfloat16)
+def dot3(a,hi,lo,cb):
+    ah,al=split(a)
+    def one(x,y): return lax.dot_general(x,y,(((1,),(cb,)),((),())),preferred_element_type=f32)
+    return one(ah,hi)+(one(ah,lo)+one(al,hi))
 def mm_tn(a,b): return dg(a,b,0,0)
 
-def chol_pieces(T, ms, put, SP=32):
+def chol_pieces(T, ms, put, SP=64):
     lane=lax.broadcasted_iota(jnp.int32,(8,128),1)
     sub=lax.broadcasted_iota(jnp.int32,(8,128),0)
     NP=SP//8
@@ -70,9 +77,8 @@
                     Yr=[jnp.broadcast_to(W[j:j+1],(8,128)) for j in range(8)]
                     for o in range(q+1,NP):
                         A=R[n][o]
-                        acc=jnp.where(inblk,0.0,A)
-                        for j in range(8):
-                            acc=acc-jnp.broadcast_to(jnp.sum(jnp.where(lane==base+j,A,0.0),axis=1,keepdims=True),(8,128))*Yr[j]
+                        t=[jnp.broadcast_to(jnp.sum(jnp.where(lane==base+j,A,0.0),axis=1,keepdims=True),(8,128))*Yr[j] for j in range(8)]
+                        acc=jnp.where(inblk,0.0,A)-(((t[0]+t[1])+(t[2]+t[3]))+((t[4]+t[5])+(t[6]+t[7])))
                         R[n][o]=acc
             yield
         if s+SP<128:
@@ -86,7 +92,7 @@
                 T[m,s+SP:,:]=jnp.where(ins,0.0,T[m,s+SP:,:])-mm(jnp.transpose(F)[s+SP:],F2)
             yield
 
-def chol_inverse(T, ms, put, fill=(), pieces=19):
+def chol_inverse(T, ms, put, fill=(), pieces=17):
     fill=list(fill)
     for i,_ in enumerate(chol_pieces(T,ms,put)):
         take=-(-len(fill)//max(pieces-i,1))
@@ -102,7 +108,7 @@
     ident=nbr[b,k]; used=ident>=0; safe=jnp.where(used,ident,0)
     return used,safe//2,safe%2
 
-def factor_body(nbr_hbm, recv0, own_hbm, fac, g4, gd, d0, send, own, nbr_v, X, T, G, coef, nbr, sems):
+def factor_body(nbr_hbm, recv0, own_hbm, fac_hi, fac_lo, g4, gd, d0, send, own, nbr_v, X, T, G, coef, nbr, sems):
     pairs=[(nbr_hbm,nbr),(own_hbm,own),(nbr_hbm,nbr_v)]
     copies=[pltpu.make_async_copy(a,b,sems.at[i]) for i,(a,b) in enumerate(pairs)]
     for c in copies: c.start()
@@ -143,17 +149,13 @@
             r,c=at(n,n)
             T[b]=X[b,r,c]-mm_nt(L,L)
         for b in range(2):
-            def rest(b=b,k=k,n=n):
-                if n<4:
-                    lo=(n+1)*128
-                    X[b,lo:,k*128:n*128]=mm_nt(X[b,lo:,k*128:n*128],G[k,b])
-            def column(j,b=b,k=k,n=n):
-                lo=max(j,n+1)*128
-                c=slice(k*128,n*128)
-                X[b,lo:,j*128:(j+1)*128]=X[b,lo:,j*128:(j+1)*128]-mm_nt(X[b,lo:,c],X[b,j*128:(j+1)*128,c])
+            lo=(n+1)*128
             if n<4:
-                fill.append(rest)
-                for j in range(n,5): fill.append(lambda j=j,column=column: column(j))
+                X[b,lo:,k*128:n*128]=mm_nt(X[b,lo:,k*128:n*128],G[k,b])
+                for j in range(n,5):
+                    o=max(j,n+1)*128
+                    c=slice(k*128,n*128)
+                    X[b,o:,j*128:(j+1)*128]=X[b,o:,j*128:(j+1)*128]-mm_nt(X[b,o:,c],X[b,j*128:(j+1)*128,c])
     dn=[]
     for b in range(2):
         d=1.0/own[2:3,b*128:(b+1)*128]; dn.append(d)
@@ -172,7 +174,7 @@
     chol_inverse(T,[0,1,2,3],put4,fill)
     ds=[]
     for b in range(2):
-        fac[b]=mm(g4[b],coef[b])
+        fac_hi[b],fac_lo[b]=split(mm(g4[b],coef[b]))
         w=own[8:24,b*128:(b+1)*128]*dn[b]
         d=w-mm(mm_nt(w,gd[b]),gd[b])*dn[b]
         d0[b]=d
@@ -218,7 +220,7 @@
                 out[pl.ds(5 * dev + 4, 1), :] = jnp.full((1, BS), which.astype(f32), f32)
 
 
-def apply_body(rows, nbr, v, recv, fac, g4, args, *rest):
+def apply_body(rows, nbr, v, recv, fac_hi, fac_lo, g4, args, *rest):
     if rows == RHS:
         q_out, part_out, send = rest
         send[...] = jnp.zeros((NDEV * RHS, BS), f32)
@@ -230,11 +232,11 @@
     for b in range(2):
         near = jnp.concatenate([recv[pl.ds(pl.multiple_of(RHS * s[1], 8), RHS), :] for s in slots[b]], 1)
         own = v[b]
-        t = mm_nt(own, g4[b]) - mm_nt(near, fac[b])
+        t = mm_nt(own, g4[b]) - dot3(near, fac_hi[b], fac_lo[b], 1)
         q = mm(t, g4[b])
         part = part + t * t + args[2:3, b * BS : (b + 1) * BS] * own * own
         q_out[b] = q
-        backs.append(-mm(t, fac[b]))
+        backs.append(-dot3(t, fac_hi[b], fac_lo[b], 0))
     if rows == RHS:
         part_out[...] = part
     else:
@@ -339,12 +341,15 @@
         name="announce",
     )(neighbors.T, locations, noise_precision.reshape(1, 2 * BS), right_side)
     recv0 = exchange(send0, 5)
-    shapes = [(2, BS, KMAX * BS), sq, sq, blk, (NDEV * RHS, BS), (24, 2 * BS)]
-    fac, g4, gd, d0, send1, own, nbr = pl.pallas_call(
+    wide = jax.ShapeDtypeStruct((2, BS, KMAX * BS), jnp.bfloat16)
+    shapes = [sq, sq, blk, (NDEV * RHS, BS), (24, 2 * BS)]
+    fac_hi, fac_lo, g4, gd, d0, send1, own, nbr = pl.pallas_call(
         factor_body,
         in_specs=[hbm, VM, hbm],
-        out_specs=[VM] * 7,
-        out_shape=[jax.ShapeDtypeStruct(s, f32) for s in shapes] + [jax.ShapeDtypeStruct((2, KMAX), jnp.int32)],
+        out_specs=[VM] * 8,
+        out_shape=[wide, wide]
+        + [jax.ShapeDtypeStruct(s, f32) for s in shapes]
+        + [jax.ShapeDtypeStruct((2, KMAX), jnp.int32)],
         scratch_shapes=[
             pltpu.VMEM((2, 640, 640), f32),
             pltpu.VMEM((4, BS, BS), f32),
@@ -358,16 +363,16 @@
     )(neighbors.T, recv0, own0)
     recv1 = exchange(send1, RHS)
     q0, apart, send2 = call(
-        lambda *r: apply_body(RHS, *r), [blk, (RHS, BS), (NDEV * RHS, BS)], 6, smem=1, name="apply_first"
-    )(nbr, d0, recv1, fac, g4, own)
+        lambda *r: apply_body(RHS, *r), [blk, (RHS, BS), (NDEV * RHS, BS)], 7, smem=1, name="apply_first"
+    )(nbr, d0, recv1, fac_hi, fac_lo, g4, own)
     recv2 = exchange(send2, RHS)
     im0, y, parts, send3 = call(
         middle_body, [blk, blk, (3, RHS, BS), (NDEV * RHS, BS)], 7, name="middle"
     )(recv0, recv2, q0, d0, own, gd, apart)
     recv3 = exchange(send3, RHS)
     q1, send4 = call(
-        lambda *r: apply_body(RHS + 1, *r), [blk, (NDEV * (RHS + 1), BS)], 7, smem=1, name="apply_second"
-    )(nbr, y, recv3, fac, g4, own, parts)
+        lambda *r: apply_body(RHS + 1, *r), [blk, (NDEV * (RHS + 1), BS)], 8, smem=1, name="apply_second"
+    )(nbr, y, recv3, fac_hi, fac_lo, g4, own, parts)
     recv4 = exchange(send4, RHS + 1)
     return tuple(
         call(last_body, [(RHS, 2 * BS)] * 2, 7, name="last")(

time: 156 us -> 154 us (0.987)
  Pallas kernels: 35.7 us -> 33.9 us
where the time goes in v3:
time: 154 us
  blocking collectives  118 us (77%)
  Pallas kernels  33.9 us (22%)
    all_to_all x5, blocking collectives, exchange(): lax.all_to_all(msg.reshape(NDEV, 1, rows * BS), 'blk', 0, 0, tiled=True)  118 us
    pallas_call x1, Pallas kernels, per_device(): pl.pallas_call(factor_body, in_specs=[hbm, VM, hbm], out_specs=[VM] * 8,...  26.5 us

profile of v3, /device:TPU:1, one launch (start us, length us, event | category | flops | bytes accessed | tf_op | source)
XLA Modules:
  0.0 153.8 jit_solution(3441901205971348213)
XLA Ops:
  0.6 1.7 %announce.1 = (f32[640,128]{1,0:T(8,128)}, f32[24,256]{1,0:T(8,128)}) custom-call(s32[2,4]{1,0:T(2,128)} %bitcast.23, f32[2,256]{1,0:T(2,128)} %loc_hbm.1, f32[1,256]{1,0:T(1,128)} %bitcast.26, f32[16,256]{1,0:T(8,128)} %rhs_hbm.1), custom_call_target="tpu_custom_call" | custom-call | tf_op jit(solution)/shard_map/announce/pallas_call | solution.py:335
  2.3 22.9 %all_to_all.25 = f32[128,1,640]{2,1,0:T(1,128)S(1)} all-to-all(f32[128,1,640]{2,1,0:T(1,128)} %bitcast.25), channel_id=1, replica_groups=mesh['blk'=128] {'blk'}, dimensions={0} | all-to-all | bytes 655360 | tf_op jit(solution)/shard_map/all_to_all | solution.py:330
  25.2 0.0 copy-start
  25.2 0.7 copy-done
  25.9 0.0 copy-start.1
  26.0 0.7 copy-done.1
  26.6 26.5 %factor.1 = (bf16[2,128,512]{2,1,0:T(8,128)(2,1)S(1)}, bf16[2,128,512]{2,1,0:T(8,128)(2,1)S(1)}, f32[2,128,128]{2,1,0:T(8,128)S(1)}, f32[2,128,128]{2,1,0:T(8,12...) custom-call(s32[2,4]{1,0:T(2,128)S(1)} %bitcast.24, ...), custom_call_target="tpu_custom_call" | custom-call | tf_op jit(solution)/shard_map/factor/pallas_call | solution.py:346
  53.1 23.6 %all_to_all.26 = f32[128,1,2048]{2,1,0:T(1,128)S(1)} all-to-all(f32[128,1,2048]{2,1,0:T(1,128)S(1)} %bitcast.20), channel_id=1, replica_groups=mesh['blk'=128] {'blk'}, dimensions={0} | all-to-all | bytes 2097152 | tf_op jit(solution)/shard_map/all_to_all | solution.py:330
  76.8 1.5 apply_first.1
  78.3 23.6 %all_to_all.27 = f32[128,1,2048]{2,1,0:T(1,128)S(1)} all-to-all(f32[128,1,2048]{2,1,0:T(1,128)S(1)} %bitcast.22), channel_id=1, replica_groups=mesh['blk'=128] {'blk'}, dimensions={0} | all-to-all | bytes 2097152 | tf_op jit(solution)/shard_map/all_to_all | solution.py:330
  101.9 1.4 middle.1
  103.3 23.5 %all_to_all.28 = f32[128,1,2048]{2,1,0:T(1,128)S(1)} all-to-all(f32[128,1,2048]{2,1,0:T(1,128)S(1)} %bitcast.21), channel_id=1, replica_groups=mesh['blk'=128] {'blk'}, dimensions={0} | all-to-all | bytes 2097152 | tf_op jit(solution)/shard_map/all_to_all | solution.py:330
  126.9 1.7 %apply_second.1 = (f32[2,16,128]{2,1,0:T(8,128)S(1)}, f32[2176,128]{1,0:T(8,128)S(1)}) custom-call(s32[2,4]{1,0:T(2,128)S(1)} %get-tuple-element.23.r_0_, f32[2,16,128]{2,1,0:T(8,128)S(1)} %get-tuple-element.34.r_1_.y, f32[2048,128]{1,0:T(8,128)S(1)} %bitcast.17, bf16[2,128,512]{2,1,0:T(8,128)(2,1)S(1)} %get-tuple-element.26.r_3_, ...), custom_call_target="tpu_custom_call" | custom-call | tf_op jit(solution)/shard_map/apply_second/pallas_call | solution.py:373
  128.5 24.2 %all_to_all.29 = f32[128,1,2176]{2,1,0:T(1,128)S(1)} all-to-all(f32[128,1,2176]{2,1,0:T(1,128)S(1)} %bitcast.19), channel_id=1, replica_groups=mesh['blk'=128] {'blk'}, dimensions={0} | all-to-all | bytes 2228224 | tf_op jit(solution)/shard_map/all_to_all | solution.py:330
  152.7 1.1 last.1
Async XLA Ops:
  25.2 0.7 copy-start
  25.9 0.7 copy-start.1
